TPU v7x, 512 devices: a whole 4x4x16 slice. The times are simulated.
512 devices in a mesh: img: 64 (over y, z), lm: 8 (over x, core).
Axes of the slice: x: 4, y: 4, z: 16, core: 2. Of those that a mesh axis runs over, the one named last changes fastest.
Arguments:
- jac_point: float32 [6, 1048576], P(None, ('img', 'lm')), may hold values from -4 to 4
- jac_cam: bfloat16 [1048576, 256], P(('img', 'lm')), may hold values from -0.125 to 0.125
- resid: float32 [2, 1048576], P(None, ('img', 'lm')), may hold values from -6 to 6
- point_ids: int32 [1048576], P(('img', 'lm')), may hold values from 0 to 4095
- cam_ids: int32 [1048576], P(('img', 'lm')), may hold values from 0 to 1023
- owner_slot: int32 [1024], replicated, may hold values from 0 to 1023, each once
- damping: float32 [1], replicated, may hold values from 0.1 to 1
Outputs:
- landmark_step: float32 [3, 32768], P(None, 'lm')
- camera_gradient: float32 [1024, 128], P(('img', 'lm'))
All inputs are finite; a program needn't handle non-finite values.
Results may differ from a plain program's by a relative error of at most 0.0029.
Values sent between devices are 32-bit elements; how exact they have to be, the bound alone decides.
No kernel may reach another device: no remote copies, remote signals or barrier semaphores. Data moves between devices by JAX's collectives and lax.ppermute only.
A program may use at most 64 MiB of HBM per device.

v0:
```python
import jax
import jax.numpy as jnp
from jax import lax
from jax.sharding import PartitionSpec as P

CAMP = 128
BLOCK = 64
LM_BLOCKS = 64


def obs_terms(jac_point, resid):
    u0, u1, u2 = (jac_point[0], jac_point[1], jac_point[2])
    v0, v1, v2 = (jac_point[3], jac_point[4], jac_point[5])
    ru, rv = (resid[0], resid[1])
    return jnp.stack(
        [
            u0 * u0 + v0 * v0,
            u0 * u1 + v0 * v1,
            u0 * u2 + v0 * v2,
            u1 * u1 + v1 * v1,
            u1 * u2 + v1 * v2,
            u2 * u2 + v2 * v2,
            u0 * ru + v0 * rv,
            u1 * ru + v1 * rv,
            u2 * ru + v2 * rv,
        ],
        axis=1,
    )


def solve_points(stats, damping):
    factor = damping[0]
    h01, h02, h12 = (stats[1], stats[2], stats[4])
    a00 = stats[0] + factor * (stats[0] + 1.0)
    a11 = stats[3] + factor * (stats[3] + 1.0)
    a22 = stats[5] + factor * (stats[5] + 1.0)
    g0, g1, g2 = (stats[6], stats[7], stats[8])
    c00 = a11 * a22 - h12 * h12
    c01 = h02 * h12 - h01 * a22
    c02 = h01 * h12 - h02 * a11
    c11 = a00 * a22 - h02 * h02
    c12 = h01 * h02 - a00 * h12
    c22 = a00 * a11 - h01 * h01
    determ = a00 * c00 + h01 * c01 + h02 * c02
    s0 = -(c00 * g0 + c01 * g1 + c02 * g2) / determ
    s1 = -(c01 * g0 + c11 * g1 + c12 * g2) / determ
    s2 = -(c02 * g0 + c12 * g1 + c22 * g2) / determ
    return jnp.stack([s0, s1, s2], axis=0)


def per_device(jac_point, jac_cam, resid, point_ids, cam_ids, owner_slot, damping):
    slice_points = LM_BLOCKS * BLOCK
    terms = obs_terms(jac_point, resid)
    local_stats = jax.ops.segment_sum(terms, point_ids, num_segments=slice_points).T
    stats = lax.psum(local_stats, "img")
    step = solve_points(stats, damping)
    step_obs = jnp.take(step, point_ids, axis=1)
    cu = (
        resid[0]
        + jac_point[0] * step_obs[0]
        + jac_point[1] * step_obs[1]
        + jac_point[2] * step_obs[2]
    )
    cv = (
        resid[1]
        + jac_point[3] * step_obs[0]
        + jac_point[4] * step_obs[1]
        + jac_point[5] * step_obs[2]
    )
    cu_half = cu.astype(jnp.bfloat16)
    cv_half = cv.astype(jnp.bfloat16)
    slots = jnp.take(owner_slot, cam_ids)
    groups_all = owner_slot.shape[0]
    n_obs = cam_ids.shape[0]
    width = min(1024, n_obs)
    group_iota = jnp.arange(groups_all, dtype=jnp.int32)[:, None]
    partial_grad = jnp.zeros((groups_all, CAMP), jnp.float32)
    for block_index in range(n_obs // width):
        lo_row = block_index * width
        block_slots = slots[lo_row : lo_row + width]
        member = (block_slots[None, :] == group_iota).astype(jnp.bfloat16)
        left_u = member * cu_half[None, lo_row : lo_row + width]
        left_v = member * cv_half[None, lo_row : lo_row + width]
        cam_block = jac_cam[lo_row : lo_row + width]
        partial_grad = partial_grad + jnp.dot(
            left_u, cam_block[:, :CAMP], preferred_element_type=jnp.float32
        )
        partial_grad = partial_grad + jnp.dot(
            left_v, cam_block[:, CAMP:], preferred_element_type=jnp.float32
        )
    gradient = lax.psum_scatter(partial_grad, ("img", "lm"), scatter_dimension=0, tiled=True)
    return (step, gradient)


def solution(mesh):
    placed = (
        P(None, ("img", "lm")),
        P(("img", "lm"), None),
        P(None, ("img", "lm")),
        P(("img", "lm")),
        P(("img", "lm")),
        P(),
        P(),
    )
    return jax.shard_map(
        per_device,
        mesh=mesh,
        in_specs=placed,
        out_specs=(P(None, "lm"), P(("img", "lm"), None)),
        check_vma=False,
    )
```

profile of v0, /device:TPU:4, one launch (start us, length us, event | category | flops | bytes accessed | tf_op | source)
XLA Modules:
  0.0 778.8 jit_solution(16912296263779753748)
XLA Ops:
  7.2 0.0 all-reduce.4.cloned.1.call-start
  7.2 1.1 add_bitcast_fusion.5
  8.4 1.2 add_bitcast_fusion
  9.5 0.1 stack.4
  9.7 0.4 copy.119
  10.0 12.1 %scatter_custom_fusion = f32[4096,9]{1,0:T(8,128)S(1)} fusion(s32[2048]{0:T(1024)} %param.10, f32[2048,9]{1,0:T(8,128)S(1)} %copy.119, f32[]{:T(128)} %constant.30.clone.1), kind=kCustom, calls=%fused_computation.28 | custom fusion | flops 18432 | bytes 147968 | tf_op jit(solution)/shard_map/scatter-add | solution.py:54
  22.1 1.3 copy.120
  23.5 0.0 all-reduce.4.cloned.1.call-update
  23.5 0.0 all-reduce.6.cloned.1.call-start
  24.2 8.6 %gather_fusion = s32[2048]{0:T(1024)S(1)} fusion(s32[1024]{0:T(1024)S(1)} %copy-done, s32[2048]{0:T(1024)S(1)} %fusion.39), kind=kCustom, calls=%fused_computation | custom fusion | bytes 24576 | tf_op jit(solution)/shard_map/jit(_take)/gather | solution.py:72
  32.9 261.6 %all-reduce.4.cloned.1.call-done = f32[9,4096]{1,0:T(8,128)} async-done(((f32[9,4096]{1,0:T(8,128)}), f32[9,4096]{1,0:T(8,128)}) %all-reduce.4.cloned.1.call-update) | async-done | bytes 147472 | tf_op jit(solution)/shard_map/psum | solution.py:55
  294.5 1.7 negate_divide_fusion.2
  296.3 1.8 negate_divide_fusion.1
  298.1 0.6 copy.121
  298.8 5.5 gather_fusion.1
  304.2 0.3 copy.122
  304.6 0.1 add_convert_fusion
  304.7 0.1 slice_reduce_fusion
  304.8 1.7 fusion.4
  306.5 0.7 fusion.22
  307.2 0.7 fusion.19
  308.0 1.5 fusion.16
  309.5 461.2 %all-reduce.6.cloned.1.call-done = f32[1024,128]{1,0:T(8,128)} async-done(((f32[1024,128]{1,0:T(8,128)}), f32[1024,128]{1,0:T(8,128)}) %all-reduce.6.cloned.1.call-update) | async-done | bytes 524304
  770.7 1.2 constant_dynamic-slice_fusion
  (22 shorter events, 0.2 us)
Async XLA Ops:
  7.2 17.1 %copy-start = (s32[1024]{0:T(1024)S(1)}, s32[1024]{0:T(1024)}, u32[]{:S(2)}) copy-start(s32[1024]{0:T(1024)} %param.12) | copy-start | bytes 12292
  7.2 287.4 %all-reduce.4.cloned.1.call-start = ((), (), s32[]{:S(2)}) async-start(), calls=%async_computation | async-start | bytes 524288 | tf_op jit(solution)/shard_map/psum | solution.py:55
  10.0 13.5 %copy-start.5 = (s32[2048]{0:T(1024)S(1)}, s32[2048]{0:T(1024)}, u32[]{:S(2)}) copy-start(s32[2048]{0:T(1024)} %param.10) | copy-start | bytes 24580
  10.0 14.2 %copy-start.4 = (s32[2048]{0:T(1024)S(1)}, s32[2048]{0:T(1024)}, u32[]{:S(2)}) copy-start(s32[2048]{0:T(1024)} %param.11) | copy-start | bytes 24580
  23.5 747.2 %all-reduce.6.cloned.1.call-start = ((), (), s32[]{:S(2)}) async-start(), calls=%async_computation.1 | async-start | bytes 1048576
  32.8 271.8 %copy-start.1 = (f32[6,2048]{1,0:T(8,128)S(1)}, f32[6,2048]{1,0:T(8,128)}, u32[]{:S(2)}) copy-start(f32[6,2048]{1,0:T(8,128)} %param.7) | copy-start | bytes 147460
  32.9 271.8 %copy-start.3 = (f32[2,2048]{1,0:T(2,128)S(1)}, f32[2,2048]{1,0:T(2,128)}, u32[]{:S(2)}) copy-start(f32[2,2048]{1,0:T(2,128)} %param.9) | copy-start | bytes 49156
  298.1 8.4 %copy-start.2 = (f32[3,4096]{1,0:T(4,128)}, f32[3,4096]{1,0:T(4,128)S(1)}, u32[]{:S(2)}) copy-start(f32[3,4096]{1,0:T(4,128)S(1)} %pad_maximum_fusion) | copy-start | bytes 147460
  304.7 1.8 copy-start.6
Sparse Core Ops, SparseCore 0:
  23.6 270.8 all-reduce.3
  309.6 461.0 all-reduce.5
where the time goes:
time: 779 us
  waiting for transfers between devices  723 us (93%)
  local copies, waits for them, and re-layouts  18.2 us (2%)
  other arithmetic  18.1 us (2%)
  between operations  14.9 us (2%)
    unnamed x3, waiting for transfers between devices  461 us
    psum x1, waiting for transfers between devices, per_device(): stats = lax.psum(local_stats, 'img')  262 us
  transfers between devices with their start and end apart: 2, of which 2 were waited for; matrix products, arithmetic and copies ran while one was open for 1% of the time, Pallas kernels for 0%

commit v1 on v0

--- a/solution.py
+++ b/solution.py
@@ -52,7 +52,8 @@
     slice_points = LM_BLOCKS * BLOCK
     terms = obs_terms(jac_point, resid)
     local_stats = jax.ops.segment_sum(terms, point_ids, num_segments=slice_points).T
-    stats = lax.psum(local_stats, "img")
+    parts = lax.all_gather(local_stats, "img")
+    stats = jnp.sum(parts, axis=0)
     step = solve_points(stats, damping)
     step_obs = jnp.take(step, point_ids, axis=1)
     cu = (

time: 779 us -> 711 us (0.913)
  waiting for transfers between devices: 723 us -> 651 us
    psum x1 -> x0, waiting for transfers between devices: 262 us -> none  [per_device(): stats = lax.psum(local_stats, 'img')]
    all_gather x0 -> x1, waiting for transfers between devices: none -> 188 us  [per_device(): parts = lax.all_gather(local_stats, 'img')]
where the time goes in v1:
time: 711 us
  waiting for transfers between devices  651 us (92%)
  other arithmetic  21.9 us (3%)
  local copies, waits for them, and re-layouts  18.2 us (3%)
  between operations  14.9 us (2%)
    unnamed x3, waiting for transfers between devices  463 us
    all_gather x1, waiting for transfers between devices, per_device(): parts = lax.all_gather(local_stats, 'img')  188 us
  transfers between devices with their start and end apart: 2, of which 2 were waited for; matrix products, arithmetic and copies ran while one was open for 1% of the time, Pallas kernels for 0%

profile of v1, /device:TPU:4, one launch (start us, length us, event | category | flops | bytes accessed | tf_op | source)
XLA Modules:
  0.0 710.7 jit_solution(2357913751743429483)
XLA Ops:
  7.2 0.0 all-gather.4.cloned.1.call-start
  7.2 1.1 add_bitcast_fusion.5
  8.4 1.2 add_bitcast_fusion
  9.6 0.1 stack.4
  9.7 0.4 copy.95
  10.1 12.1 %scatter_custom_fusion = f32[4096,9]{1,0:T(8,128)S(1)} fusion(s32[2048]{0:T(1024)} %param.10, f32[2048,9]{1,0:T(8,128)S(1)} %copy.95, f32[]{:T(128)} %constant.31.clone.1), kind=kCustom, calls=%fused_computation.28 | custom fusion | flops 18432 | bytes 147968 | tf_op jit(solution)/shard_map/scatter-add | solution.py:54
  22.2 1.3 copy.96
  23.5 0.0 all-reduce.3.cloned.1.call-start
  24.3 8.6 %gather_fusion = s32[2048]{0:T(1024)S(1)} fusion(s32[1024]{0:T(1024)S(1)} %copy-done, s32[2048]{0:T(1024)S(1)} %fusion.39), kind=kCustom, calls=%fused_computation | custom fusion | bytes 24576 | tf_op jit(solution)/shard_map/jit(_take)/gather | solution.py:73
  32.9 188.1 %all-gather.4.cloned.1.call-done = f32[64,9,4096]{2,1,0:T(8,128)} async-done(((f32[1,9,4096]{2,1,0:T(8,128)}), f32[64,9,4096]{2,1,0:T(8,128)}) %all-gather.4.cloned.1.call-update) | async-done | bytes 9437200 | tf_op jit(solution)/shard_map/all_gather | solution.py:55
  221.0 6.9 reduce_sum.9
  227.9 0.2 negate_divide_fusion.2
  228.1 0.2 negate_divide_fusion.1
  228.4 0.6 copy.97
  229.1 5.5 gather_fusion.1
  234.5 0.3 copy.98
  234.9 0.1 add_convert_fusion
  235.0 0.1 slice_reduce_fusion
  235.1 1.7 fusion.4
  236.8 0.7 fusion.22
  237.6 0.7 fusion.19
  238.3 1.5 fusion.16
  239.8 462.8 %all-reduce.3.cloned.1.call-done = f32[1024,128]{1,0:T(8,128)} async-done(((f32[1024,128]{1,0:T(8,128)}), f32[1024,128]{1,0:T(8,128)}) %all-reduce.3.cloned.1.call-update) | async-done | bytes 524304
  702.7 1.2 constant_dynamic-slice_fusion
  (23 shorter events, 0.2 us)
Async XLA Ops:
  7.2 17.1 %copy-start = (s32[1024]{0:T(1024)S(1)}, s32[1024]{0:T(1024)}, u32[]{:S(2)}) copy-start(s32[1024]{0:T(1024)} %param.12) | copy-start | bytes 12292
  7.2 213.8 %all-gather.4.cloned.1.call-start = ((), (), s32[]{:S(2)}) async-start(), calls=%async_computation | async-start | bytes 17039360 | tf_op jit(solution)/shard_map/all_gather | solution.py:55
  10.1 14.2 %copy-start.4 = (s32[2048]{0:T(1024)S(1)}, s32[2048]{0:T(1024)}, u32[]{:S(2)}) copy-start(s32[2048]{0:T(1024)} %param.11) | copy-start | bytes 24580
  23.5 679.1 %all-reduce.3.cloned.1.call-start = ((), (), s32[]{:S(2)}) async-start(), calls=%async_computation.1 | async-start | bytes 1048576
  24.3 8.6 %copy-start.5 = (s32[2048]{0:T(1024)S(1)}, s32[2048]{0:T(1024)}, u32[]{:S(2)}) copy-start(s32[2048]{0:T(1024)} %param.10) | copy-start | bytes 24580
  227.9 7.0 copy-start.1
  227.9 7.0 copy-start.3
  228.4 8.4 %copy-start.2 = (f32[3,4096]{1,0:T(4,128)}, f32[3,4096]{1,0:T(4,128)S(1)}, u32[]{:S(2)}) copy-start(f32[3,4096]{1,0:T(4,128)S(1)} %pad_maximum_fusion) | copy-start | bytes 147460
  235.1 1.8 copy-start.6
Sparse Core Ops, SparseCore 0:
  23.7 197.3 all-gather.3
  239.9 462.6 all-reduce.2
